TPU v7x, 32 devices: a whole 2x2x4 slice. The times are simulated.
32 devices in a mesh: row: 4 (over y, x), col: 8 (over z, core).
Axes of the slice: x: 2, y: 2, z: 4, core: 2. Of those that a mesh axis runs over, the one named last changes fastest.
Arguments:
- wavefield: bfloat16 [2, 1, 8192, 8192], P(None, None, 'row', 'col'), as said below
- panel_order: int32 [16], replicated, may hold values from 0 to 15, each once
- filter_taps: float32 [11, 8192], P(None, 'col'), may hold values from -4 to 4
Outputs:
- primaries: bfloat16 [2, 1, 8192, 8192], P(None, None, 'row', 'col')
Inputs may be any that keep to these rules, and one draw needn't show every extreme that they name: Reciprocity: wavefield[c, f, s, r] = wavefield[c, f, r, s] for every part, frequency, shot and receiver.
All inputs are finite; a program needn't handle non-finite values.
Results may differ from a plain program's by a relative error of at most 0.00045.
Values may be sent and summed in bfloat16 or wider, within the bound.
A program may use at most 128 MiB of HBM per device.

v0:
```python
import math

import jax
import jax.numpy as jnp
from jax import lax
from jax.sharding import PartitionSpec as P

SIDE = 8192
PANEL = 512
STEPS = 3
TAPS = 11
FIRST_FREQUENCY = 8
NT = 1024


def spread(block, axis, holder):
    block = jnp.where(lax.axis_index(axis) == holder, block, jnp.zeros_like(block))
    return lax.psum(block, axis)


def frequency_spectrum(filter_taps, freq_count):
    lags = jnp.arange(TAPS, dtype=jnp.float32)
    omega = 2.0 * math.pi * (FIRST_FREQUENCY + jnp.arange(freq_count, dtype=jnp.float32)) / NT
    phase = omega[:, None] * lags[None, :]
    real_part = jnp.dot(jnp.cos(phase), filter_taps, precision=lax.Precision.HIGHEST)
    imag_part = -jnp.dot(jnp.sin(phase), filter_taps, precision=lax.Precision.HIGHEST)
    return (real_part, imag_part)


def local(wavefield, panel_order, filter_taps):
    freq_count = wavefield.shape[1]
    shot_block = wavefield.shape[2]
    recv_block = wavefield.shape[3]
    own_row_index = lax.axis_index("row")
    factor = 1.0 / math.sqrt(STEPS * PANEL)
    count = 2.0 * SIDE * SIDE
    local_data = jnp.sum(jnp.square(wavefield.astype(jnp.float32)), axis=(0, 2, 3))
    energy_data = lax.psum(local_data, ("row", "col"))
    totals = jnp.zeros((freq_count, shot_block, 2 * recv_block), jnp.float32)
    for panel_advance in range(STEPS):
        first_point = panel_order[panel_advance] * PANEL
        row_width = min(PANEL, shot_block)
        owner_turn = 0
        start = first_point + owner_turn * row_width
        piece = lax.dynamic_slice_in_dim(wavefield, start % shot_block, row_width, 2)
        row_pieces = spread(piece, "row", start // shot_block)
        col_pieces = []
        mirror_width = min(shot_block, recv_block)
        for owner_turn in range(max(1, shot_block // recv_block)):
            start = own_row_index * shot_block + owner_turn * mirror_width
            piece = row_pieces
            col_pieces.append(spread(piece, "col", start // recv_block))
        upper = jnp.swapaxes(jnp.concatenate(col_pieces, axis=3), 2, 3)
        left_factor = jnp.concatenate([upper[0], upper[1]], axis=2)
        right_factor = jnp.concatenate(
            [
                jnp.concatenate([row_pieces[0], row_pieces[1]], axis=2),
                jnp.concatenate([-row_pieces[1], row_pieces[0]], axis=2),
            ],
            axis=1,
        )
        totals = totals + jnp.einsum(
            "yga,yah->ygh", left_factor, right_factor, preferred_element_type=jnp.float32
        )
    mult_re = totals[:, :, :recv_block] * factor
    mult_im = totals[:, :, recv_block:] * factor
    local_mult = jnp.sum(mult_re * mult_re, axis=(1, 2)) + jnp.sum(mult_im * mult_im, axis=(1, 2))
    energy_mult = lax.psum(local_mult, ("row", "col"))
    gain = jnp.sqrt((energy_data / count + 1e-05) / (energy_mult / count + 1e-05))[:, None, None]
    spec_re, spectrum_imaginary = frequency_spectrum(filter_taps, freq_count)
    a_re = spec_re[:, None, :]
    a_im = spectrum_imaginary[:, None, :]
    sub_re = gain * (a_re * mult_re - a_im * mult_im)
    subtracted_imaginary = gain * (a_re * mult_im + a_im * mult_re)
    result = jnp.stack(
        [
            wavefield[0].astype(jnp.float32) - sub_re,
            wavefield[1].astype(jnp.float32) - subtracted_imaginary,
        ]
    )
    return result.astype(jnp.bfloat16)


def solution(mesh):
    in_specs = (P(None, None, "row", "col"), P(), P(None, "col"))
    out_specs = P(None, None, "row", "col")
    return jax.shard_map(local, mesh=mesh, in_specs=in_specs, out_specs=out_specs, check_vma=False)
```

profile of v0, /device:TPU:0, one launch (start us, length us, event | category | flops | bytes accessed | tf_op | source)
XLA Modules:
  0.0 574.5 jit_solution(4812918331580029134)
XLA Ops:
  6.5 1.4 fusion.46
  9.9 6.9 %dynamic-slice_select_fusion = (bf16[2,1,512,1024]{3,2,1,0:T(8,128)(2,1)}, bf16[2,1,512,1024]{3,2,1,0:T(8,128)(2,1)}, bf16[2,1,512,1024]{3,2,1,0:T(8,128)(2,1)}) fusion(bf16[2,1,2048,1024]{3,2,1,0:T(8,128)(2,1)} %param.3, s32[]{:T(128)S(6)} %select_n.113, pred[]{:T(512)S(6)} %eq.27, s32[]{:T(128)S(6)} %select_n.106, pred[]{:T(512)S(6)} %eq.26, ...), kind=kLoop, calls=%fused_computation.52 | loop fusion | flops 3145728 | bytes 12582927 | tf_op jit(solution)/shard_map/jit(_where)/select_n | solution.py:17
  16.9 0.2 all-reduce.6.cloned.1.call-start
  17.1 140.8 %all-reduce.8.cloned.1.call-done = (bf16[2,1,512,1024]{3,2,1,0:T(8,128)(2,1)}, bf16[2,1,512,1024]{3,2,1,0:T(8,128)(2,1)}, bf16[2,1,512,1024]{3,2,1,0:T(8,128)(2,1)}) async-done(((bf16[2,1,512,1024]{3,2,1,0:T(8,128)(2,1)}, bf16[2,1,512,1024]{3,2,1,0:T(8,128)(2,1)}, bf16[2,1,512,1024]{3,2,1,0:T(8,128)(2,1)}), (bf16[2,1,512,1024]{3,2,1,0:T(8,128)(2,1)}, bf16[2,1,512,1024]{3,2,1,0:T(8,128)(2,1)}, ...) | async-done | bytes 6291472 | tf_op jit(solution)/shard_map/psum | solution.py:18
  157.9 4.0 broadcast_select_fusion.5
  162.0 3.5 broadcast_select_fusion.3
  165.5 0.2 fusion.30
  165.7 0.2 fusion.32
  165.9 8.5 %multiply_reduce_fusion = f32[]{:T(128)} fusion(bf16[2,1,2048,1024]{3,2,1,0:T(8,128)(2,1)} %param.3), kind=kLoop, calls=%fused_computation.1 | loop fusion | flops 12582911 | bytes 8388612 | tf_op jit(solution)/shard_map/reduce_sum | solution.py:37
  174.4 0.1 fusion.45
  174.5 1.6 slice_bitcast_fusion.10
  176.0 0.7 copy-done.4
  176.7 1.6 fusion.43
  178.4 2.1 slice_bitcast_fusion.6
  180.5 239.8 %all-reduce.6.cloned.1.call-done = (bf16[2,1,512,1024]{3,2,1,0:T(8,128)(2,1)}, bf16[2,1,512,1024]{3,2,1,0:T(8,128)(2,1)}, bf16[2,1,512,1024]{3,2,1,0:T(8,128)(2,...) async-done(((bf16[2,1,512,1024]{3,2,1,0:T(8,128)(2,1)}, bf16[2,1,512,1024]{3,2,1,0:T(8,128)(2,1)}, ...) | async-done | bytes 12582928 | tf_op jit(solution)/shard_map/psum | solution.py:18
  420.3 2.7 maximum_bitcast_fusion
  423.1 0.3 slice_bitcast_fusion.5
  423.4 1.3 copy-done.8
  424.6 0.6 copy-done.9
  425.3 0.4 maximum_bitcast_fusion.5
  425.7 0.6 slice_bitcast_fusion.3
  426.3 1.0 copy-done.6
  427.3 0.6 copy-done.7
  427.9 0.4 maximum_bitcast_fusion.10
  428.4 0.6 slice_bitcast_fusion.1
  429.0 14.7 %fusion.13 = f32[2048,2048]{1,0:T(8,128)} fusion(bf16[1,2048,512]{1,2,0:T(8,128)(2,1)S(1)} %get-tuple-element.26, bf16[1,2048,512]{1,2,0:T(8,128)(2,1)S(1)} %get-tuple-element.25, bf16[1,512,1024]{2,1,0:T(8,128)(2,1)} %get-tuple-element.46, bf16[1,512,1024]{2,1,0:T(8,128)(2,1)} %get-tuple-element.49, bf16[1,512,1024]{2,1,0:T(8,128)(2,1)} %get-tuple-element.47), kind=kOutput, calls=%fused_computation.25 | convolution fusion | flops 8615100416 | bytes 24117248 | tf_op jit(solution)/shard_map/yga,yah->ygh/dot_general | solution.py:62
  443.8 25.3 %fusion.4 = f32[2048,2048]{1,0:T(8,128)} fusion(bf16[1,2048,512]{1,2,0:T(8,128)(2,1)S(1)} %get-tuple-element.28, bf16[1,2048,512]{1,2,0:T(8,128)(2,1)S(1)} %get-tuple-element.27, bf16[1,512,1024]{2,1,0:T(8,128)(2,1)S(1)} %copy-done.11, bf16[1,512,1024]{2,1,0:T(8,128)(2,1)S(1)} %copy-done.12, bf16[1,512,1024]{2,1,0:T(8,128)(2,1)S(1)} %copy-done.10), kind=kOutput, calls=%fused_computation.13 | convolution fusion | flops 8615100416 | bytes 24117248 | tf_op jit(solution)/shard_map/yga,yah->ygh/dot_general | solution.py:62
  469.0 29.0 %add_bitcast_fusion = f32[1,2048,2048]{2,1,0:T(8,128)} fusion(f32[2048,2048]{1,0:T(8,128)} %fusion.4, f32[2048,2048]{1,0:T(8,128)} %fusion.13, bf16[1,2048,512]{1,2,0:T(8,128)(2,1)S(1)} %get-tuple-element.24, bf16[1,2048,512]{1,2,0:T(8,128)(2,1)S(1)} %get-tuple-element.23, bf16[1,512,1024]{2,1,0:T(8,128)(2,1)S(1)} %copy-done.14, ...), kind=kOutput, calls=%fused_computation | convolution fusion | flops 8623489024 | bytes 57671680 | tf_op jit(solution)/shard_map/yga,yah->ygh/dot_general | solution.py:62
  498.0 7.5 %multiply_reduce_fusion.1 = (f32[]{:T(128)}, f32[]{:T(128)}) fusion(f32[1,2048,2048]{2,1,0:T(8,128)} %add_bitcast_fusion), kind=kLoop, calls=%fused_computation.7 | loop fusion | flops 12582910 | bytes 16777224 | tf_op jit(solution)/shard_map/reduce_sum | solution.py:67
  506.8 40.9 %all-reduce = (f32[1]{0:T(128)}, f32[1]{0:T(128)}) all-reduce(f32[1]{0:T(128)} %bitcast.1, f32[1]{0:T(128)} %bitcast.27), channel_id=1, replica_groups=mesh['row'=4,'col'=8] {'row','col'}, use_global_device_ids=true, to_apply=%region_1.0 | all-reduce | flops 2 | bytes 16 | tf_op jit(solution)/shard_map/psum | solution.py:38
  549.0 12.3 %fusion.2 = (bf16[1,1,2048,1024]{3,2,1,0:T(8,128)(2,1)S(1)}, bf16[1,1,2048,1024]{3,2,1,0:T(8,128)(2,1)}) fusion(f32[1,2048,2048]{2,1,0:T(8,128)} %add_bitcast_fusion, f32[1024]{0:T(1024)S(1)} %get-tuple-element.50, f32[1024]{0:T(1024)S(1)} %get-tuple-element.51, f32[]{:T(128)} %bitcast.28, bf16[2,1,2048,1024]{3,2,1,0:T(8,128)(2,1)} %param.3), kind=kLoop, calls=%fused_computation.9 | loop fusion | flops 29360128 | bytes 33562628 | tf_op jit(solution)/shard_map/stack | solution.py:75
  561.3 6.4 %pad_maximum_fusion = bf16[2,1,2048,1024]{3,2,1,0:T(8,128)(2,1)} fusion(bf16[1,1,2048,1024]{3,2,1,0:T(8,128)(2,1)} %get-tuple-element.19, bf16[1,1,2048,1024]{3,2,1,0:T(8,128)(2,1)S(1)} %get-tuple-element.18), kind=kLoop, calls=%fused_computation.2 | loop fusion | flops 4194304 | bytes 16777216 | tf_op jit(solution)/shard_map/stack | solution.py:75
  (29 shorter events, 0.1 us)
Async XLA Ops:
  6.5 158.9 %copy-start = (f32[11,1024]{1,0:T(8,128)S(1)}, f32[11,1024]{1,0:T(8,128)}, u32[]{:S(2)}) copy-start(f32[11,1024]{1,0:T(8,128)} %param.5) | copy-start | bytes 135172
  6.5 151.4 %all-reduce.8.cloned.1.call-start = ((), (), s32[]{:S(2)}) async-start(), calls=%async_computation.1 | async-start | bytes 12582912 | tf_op jit(solution)/shard_map/psum | solution.py:18
  16.9 403.4 %all-reduce.6.cloned.1.call-start = ((), (), s32[]{:S(2)}) async-start(), calls=%async_computation | async-start | bytes 25165824 | tf_op jit(solution)/shard_map/psum | solution.py:18
  157.9 4.0 copy-start.2
  157.9 4.0 copy-start.3
  165.9 8.5 %copy-start.5 = (bf16[2,1,512,1024]{3,2,1,0:T(8,128)(2,1)S(1)}, bf16[2,1,512,1024]{3,2,1,0:T(8,128)(2,1)}, u32[]{:S(2)}) copy-start(bf16[2,1,512,1024]{3,2,1,0:T(8,128)(2,1)} %get-tuple-element.15) | copy-start | bytes 6291460
  174.4 2.3 copy-start.4
  423.0 1.6 copy-start.8
  423.0 2.2 copy-start.9
  425.7 1.6 copy-start.6
  425.7 2.2 copy-start.7
  428.9 14.8 %copy-start.10 = (bf16[1,512,1024]{2,1,0:T(8,128)(2,1)S(1)}, bf16[1,512,1024]{2,1,0:T(8,128)(2,1)}, u32[]{:S(2)}) copy-start(bf16[1,512,1024]{2,1,0:T(8,128)(2,1)} %get-tuple-element.33) | copy-start | bytes 3145732
  429.0 14.8 %copy-start.11 = (bf16[1,512,1024]{2,1,0:T(8,128)(2,1)S(1)}, bf16[1,512,1024]{2,1,0:T(8,128)(2,1)}, u32[]{:S(2)}) copy-start(bf16[1,512,1024]{2,1,0:T(8,128)(2,1)} %get-tuple-element.34) | copy-start | bytes 3145732
  429.0 14.8 %copy-start.12 = (bf16[1,512,1024]{2,1,0:T(8,128)(2,1)S(1)}, bf16[1,512,1024]{2,1,0:T(8,128)(2,1)}, u32[]{:S(2)}) copy-start(bf16[1,512,1024]{2,1,0:T(8,128)(2,1)} %get-tuple-element.48) | copy-start | bytes 3145732
  443.7 25.3 %copy-start.13 = (bf16[1,512,1024]{2,1,0:T(8,128)(2,1)S(1)}, bf16[1,512,1024]{2,1,0:T(8,128)(2,1)}, u32[]{:S(2)}) copy-start(bf16[1,512,1024]{2,1,0:T(8,128)(2,1)} %get-tuple-element.29) | copy-start | bytes 3145732
  443.7 25.3 %copy-start.14 = (bf16[1,512,1024]{2,1,0:T(8,128)(2,1)S(1)}, bf16[1,512,1024]{2,1,0:T(8,128)(2,1)}, u32[]{:S(2)}) copy-start(bf16[1,512,1024]{2,1,0:T(8,128)(2,1)} %get-tuple-element.30) | copy-start | bytes 3145732
  561.3 6.4 %copy-start.1 = (f32[11,1024]{1,0:T(8,128)S(1)}, f32[11,1024]{1,0:T(8,128)}, u32[]{:S(2)}) copy-start(f32[11,1024]{1,0:T(8,128)} %param.5) | copy-start | bytes 135172
Sparse Core Ops, SparseCore 0:
  17.0 140.8 all-reduce.7
  165.6 254.6 all-reduce.5
where the time goes:
time: 575 us; the launch traced here: 574 us
  waiting for transfers between devices  381 us (66%)
  matrix products  69.4 us (12%)
  other arithmetic  54.4 us (9%)
  blocking collectives  40.9 us (7%)
  between operations  18.1 us (3%)
  local copies, waits for them, and re-layouts  10.8 us (2%)
    psum x2, waiting for transfers between devices, spread(): return lax.psum(block, axis)  381 us
    dot_general x3, matrix products, local(): jnp.einsum('yga,yah->ygh', left_factor, right_factor, preferred_element_t...  69 us
    psum x1, blocking collectives, local(): energy_data = lax.psum(local_data, ('row', 'col'))  40.9 us
    another operation x2, other arithmetic, local(): jnp.stack([wavefield[0].astype(jnp.float32) - sub_re, wavefield[1].astype...  18.6 us
    select_n x3, other arithmetic, spread(): jnp.where(lax.axis_index(axis) == holder, block, jnp.zeros_like(block))  14.4 us
  transfers between devices with their start and end apart: 2, of which 2 were waited for; matrix products, arithmetic and copies ran while one was open for 2% of the time, Pallas kernels for 0%

commit v1 on v0

--- a/solution.py
+++ b/solution.py
@@ -3,6 +3,8 @@
 import jax
 import jax.numpy as jnp
 from jax import lax
+from jax.experimental import pallas as pl
+from jax.experimental.pallas import tpu as pltpu
 from jax.sharding import PartitionSpec as P
 
 SIDE = 8192
@@ -11,6 +13,14 @@
 TAPS = 11
 FIRST_FREQUENCY = 8
 NT = 1024
+MESH = pl.DeviceIdType.MESH
+
+CHUNK = 64
+NCHUNK = STEPS * PANEL // CHUNK
+GROUP = 4
+NGROUP = NCHUNK // GROUP
+TILE = 256
+LAG = 5
 
 
 def spread(block, axis, holder):
@@ -81,7 +91,242 @@
     return result.astype(jnp.bfloat16)
 
 
+def predict_kernel(pieces, mult, energy, own, first, second, left, acc, right,
+                   xs, xr, ys, yr, us, ds, zr, ps, pr, own_sem, out_sem):
+    row = lax.axis_index("row")
+    col = lax.axis_index("col")
+    z = col // 2
+    core = col % 2
+    along_x = row + 1 - 2 * (row % 2)
+    along_y = (row + 2) % 4
+    partner = col + 1 - 2 * core
+    width = first.shape[3]
+    above = z - row
+    far = jnp.abs(above)
+
+    load = pltpu.make_async_copy(pieces, own, own_sem)
+    load.start()
+    barrier = pltpu.get_barrier_semaphore()
+    pl.semaphore_signal(barrier, inc=1, device_id=(along_x, col), device_id_type=MESH)
+    pl.semaphore_signal(barrier, inc=1, device_id=(along_y, col), device_id_type=MESH)
+    pl.semaphore_signal(barrier, inc=1, device_id=(row, partner), device_id_type=MESH)
+
+    @pl.when(z > 0)
+    def _():
+        pl.semaphore_signal(barrier, inc=1, device_id=(row, col - 2), device_id_type=MESH)
+
+    @pl.when(z < 3)
+    def _():
+        pl.semaphore_signal(barrier, inc=1, device_id=(row, col + 2), device_id_type=MESH)
+
+    pl.semaphore_wait(barrier, 3 + jnp.minimum(z, 1) + jnp.minimum(3 - z, 1))
+
+    def x_copy(k):
+        to = along_x + (k % 2) * (along_y - along_x)
+        return pltpu.make_async_remote_copy(
+            src_ref=pieces.at[k], dst_ref=first.at[k], send_sem=xs.at[k], recv_sem=xr.at[k],
+            device_id=(to, col), device_id_type=MESH)
+
+    def y_copy(k):
+        to = along_y + (k % 2) * (along_x - along_y)
+        return pltpu.make_async_remote_copy(
+            src_ref=first.at[k], dst_ref=second.at[k], send_sem=ys.at[k], recv_sem=yr.at[k],
+            device_id=(to, col), device_id_type=MESH)
+
+    def z_copy(src, k, to, sem):
+        return pltpu.make_async_remote_copy(
+            src_ref=src, dst_ref=left.at[core, k], send_sem=sem.at[k], recv_sem=zr.at[k],
+            device_id=(row, to), device_id_type=MESH)
+
+    def p_copy(src, k):
+        return pltpu.make_async_remote_copy(
+            src_ref=src, dst_ref=left.at[core, k], send_sem=ps.at[k], recv_sem=pr.at[k],
+            device_id=(row, partner), device_id_type=MESH)
+
+    go_up = jnp.logical_and(above >= 0, z < 3)
+    go_down = jnp.logical_and(above <= 0, z > 0)
+
+    def pass_on(src, k):
+        @pl.when(go_up)
+        def _():
+            z_copy(src, k, col + 2, us).start()
+
+        @pl.when(go_down)
+        def _():
+            z_copy(src, k, col - 2, ds).start()
+
+        p_copy(src, k).start()
+
+    @pl.loop(0, NCHUNK)
+    def _(k):
+        x_copy(k).start()
+
+    load.wait()
+
+    def out_copy(part, at):
+        return pltpu.make_async_copy(
+            acc.at[part, pl.ds(at, TILE), :], mult.at[part, pl.ds(at, TILE), :], out_sem.at[0])
+
+    @pl.loop(0, NCHUNK + LAG + GROUP - 1)
+    def _(s):
+        @pl.when(s < NCHUNK)
+        def _():
+            x_copy(s).wait_recv()
+            first[s] = first[s] + own[s]
+            y_copy(s).start()
+
+        k1 = s - 1
+
+        @pl.when(jnp.logical_and(k1 >= 0, k1 < NCHUNK))
+        def _():
+            y_copy(k1).wait_recv()
+            second[k1] = second[k1] + first[k1]
+
+            @pl.when(above == 0)
+            def _():
+                pass_on(second.at[k1], k1)
+                left[core, k1] = second[k1]
+
+        k2 = s - 1 - far
+
+        @pl.when(jnp.logical_and(far > 0, jnp.logical_and(k2 >= 0, k2 < NCHUNK)))
+        def _():
+            z_copy(second.at[k2], k2, partner, us).wait_recv()
+            pass_on(left.at[core, k2], k2)
+
+        k3 = s - LAG
+
+        @pl.when(jnp.logical_and(k3 >= 0, k3 < NCHUNK))
+        def _():
+            pltpu.make_async_remote_copy(
+                src_ref=second.at[k3], dst_ref=left.at[1 - core, k3], send_sem=ps.at[k3],
+                recv_sem=pr.at[k3], device_id=(row, partner), device_id_type=MESH).wait_recv()
+
+        step = s - (LAG + GROUP - 1)
+
+        @pl.when(step >= 0)
+        def _():
+            group = step // GROUP
+            part = step % GROUP
+
+            @pl.when(part == 0)
+            def _():
+                re = second[pl.ds(group * GROUP, GROUP), 0]
+                im = second[pl.ds(group * GROUP, GROUP), 1]
+                right[0, :, 0] = re
+                right[0, :, 1] = -im
+                right[1, :, 0] = im
+                right[1, :, 1] = re
+
+            depth = 2 * GROUP * CHUNK
+            per_half = width // TILE
+
+            @pl.loop(0, 2 * per_half // GROUP)
+            def _(i):
+                tile = part * (2 * per_half // GROUP) + i
+                half = tile // per_half
+                inner = pl.multiple_of((tile % per_half) * TILE, TILE)
+                at = pl.multiple_of(tile * TILE, TILE)
+                lhs = left[half, pl.ds(group * GROUP, GROUP), :, :, pl.ds(inner, TILE)]
+                lhs = lhs.reshape(depth, TILE)
+                for c in range(2):
+                    rhs = right[c].reshape(depth, width)
+                    got = lax.dot_general(
+                        lhs, rhs, (((0,), (0,)), ((), ())), preferred_element_type=jnp.float32)
+
+                    @pl.when(group == 0)
+                    def _():
+                        acc[c, pl.ds(at, TILE), :] = got
+
+                    @pl.when(group > 0)
+                    def _():
+                        acc[c, pl.ds(at, TILE), :] = acc[c, pl.ds(at, TILE), :] + got
+
+                @pl.when(group == NGROUP - 1)
+                def _():
+                    for c in range(2):
+                        out_copy(c, at).start()
+
+    energy[...] = jnp.zeros_like(energy)
+
+    @pl.loop(0, acc.shape[1] // 8)
+    def _(i):
+        at = pl.multiple_of(i * 8, 8)
+        re = acc[0, pl.ds(at, 8), :]
+        im = acc[1, pl.ds(at, 8), :]
+        energy[...] = energy[...] + (re * re + im * im)
+
+    pltpu.make_async_copy(acc, mult, out_sem.at[0]).wait()
+
+    @pl.loop(0, NCHUNK)
+    def _(k):
+        x_copy(k).wait_send()
+        y_copy(k).wait_send()
+        p_copy(second.at[k], k).wait_send()
+
+        @pl.when(go_up)
+        def _():
+            z_copy(second.at[k], k, col + 2, us).wait_send()
+
+        @pl.when(go_down)
+        def _():
+            z_copy(second.at[k], k, col - 2, ds).wait_send()
+
+
+def local_fast(wavefield, panel_order, filter_taps):
+    shot_block = wavefield.shape[2]
+    recv_block = wavefield.shape[3]
+    factor = 1.0 / math.sqrt(STEPS * PANEL)
+    count = 2.0 * SIDE * SIDE
+    field = wavefield[:, 0]
+    me = lax.axis_index("row")
+    parts = []
+    for t in range(STEPS):
+        start = panel_order[t] * PANEL
+        piece = lax.dynamic_slice_in_dim(field, start % shot_block, PANEL, 1)
+        piece = jnp.where(me == start // shot_block, piece, jnp.zeros_like(piece))
+        piece = piece.reshape(2, PANEL // CHUNK, CHUNK, recv_block)
+        parts.append(jnp.swapaxes(piece, 0, 1))
+    pieces = jnp.concatenate(parts, axis=0)
+    block = (NCHUNK, 2, CHUNK, recv_block)
+    dma = pltpu.SemaphoreType.DMA
+    mult, energy = pl.pallas_call(
+        predict_kernel,
+        out_shape=(
+            jax.ShapeDtypeStruct((2, shot_block, recv_block), jnp.float32),
+            jax.ShapeDtypeStruct((8, recv_block), jnp.float32),
+        ),
+        in_specs=[pl.BlockSpec(memory_space=pl.ANY)],
+        out_specs=(pl.BlockSpec(memory_space=pl.ANY), pl.BlockSpec(memory_space=pltpu.VMEM)),
+        scratch_shapes=[
+            pltpu.VMEM(block, jnp.bfloat16),
+            pltpu.VMEM(block, jnp.bfloat16),
+            pltpu.VMEM(block, jnp.bfloat16),
+            pltpu.VMEM((2,) + block, jnp.bfloat16),
+            pltpu.VMEM((2, shot_block, recv_block), jnp.float32),
+            pltpu.VMEM((2, GROUP, 2, CHUNK, recv_block), jnp.bfloat16),
+        ] + [dma((NCHUNK,))] * 9 + [dma, dma((1,))],
+        compiler_params=pltpu.CompilerParams(
+            collective_id=0, has_side_effects=True, vmem_limit_bytes=60 << 20),
+        name="predict",
+    )(pieces)
+    local_data = jnp.sum(jnp.square(field.astype(jnp.float32)))
+    both = jnp.stack([local_data, jnp.sum(energy) * (factor * factor)])
+    both = lax.psum(both, ("row", "col"))
+    gain = jnp.sqrt((both[0] / count + 1e-05) / (both[1] / count + 1e-05))
+    spec_re, spec_im = frequency_spectrum(filter_taps, 1)
+    mult_re = mult[0] * factor
+    mult_im = mult[1] * factor
+    sub_re = gain * (spec_re * mult_re - spec_im * mult_im)
+    sub_im = gain * (spec_re * mult_im + spec_im * mult_re)
+    out_re = (field[0].astype(jnp.float32) - sub_re).astype(jnp.bfloat16)
+    out_im = (field[1].astype(jnp.float32) - sub_im).astype(jnp.bfloat16)
+    return jnp.stack([out_re, out_im])[:, None]
+
+
 def solution(mesh):
     in_specs = (P(None, None, "row", "col"), P(), P(None, "col"))
     out_specs = P(None, None, "row", "col")
-    return jax.shard_map(local, mesh=mesh, in_specs=in_specs, out_specs=out_specs, check_vma=False)
+    fast = mesh.shape["row"] == 4 and mesh.shape["col"] == 8
+    body = local_fast if fast else local
+    return jax.shard_map(body, mesh=mesh, in_specs=in_specs, out_specs=out_specs, check_vma=False)

time: 575 us -> 332 us (0.58)
  waiting for transfers between devices: 381 us -> 0 us
  Pallas kernels: 0 us -> 233 us
  matrix products: 69.4 us -> 0.42 us
  other arithmetic: 54.4 us -> 38.8 us
  between operations: 18.1 us -> 4.08 us
  blocking collectives: 40.9 us -> 53 us
  local copies, waits for them, and re-layouts: 10.8 us -> 1.91 us
    psum x2 -> x0, waiting for transfers between devices: 381 us -> none  [spread(): return lax.psum(block, axis)]
    pallas_call x0 -> x1, Pallas kernels: none -> 233 us  [local_fast(): pl.pallas_call(predict_kernel, out_shape=(jax.ShapeDtypeStruct((2, shot_b...]
    dot_general x3 -> x0, matrix products: 69 us -> none  [local(): jnp.einsum('yga,yah->ygh', left_factor, right_factor, preferred_element_t...]
    another operation x2 -> x1, other arithmetic: 18.6 us -> 0.71 us  [local_fast(): both = jnp.stack([local_data, jnp.sum(energy) * (factor * factor)])]
    convert_element_type x0 -> x1, other arithmetic: none -> 12.2 us  [local_fast(): out_re = (field[0].astype(jnp.float32) - sub_re).astype(jnp.bfloat16)]
    psum x1, blocking collectives: 40.9 us -> 53 us  [local_fast(): both = lax.psum(both, ('row', 'col'))]
    select_n x3 -> x1, other arithmetic: 14.4 us -> 4.8 us  [local_fast(): piece = jnp.where(me == start // shot_block, piece, jnp.zeros_like(piece))]
    broadcast_in_dim x0 -> x1, other arithmetic: none -> 6.35 us  [local_fast(): return jnp.stack([out_re, out_im])[:, None]]
  transfers between devices with their start and end apart: 2 -> 0, of which waited for: 2 -> 0; matrix products, arithmetic and copies ran while one was open for 2% -> 0% of each run, Pallas kernels for 0% -> 0%
where the time goes in v1:
time: 332 us; the launch traced here: 331 us
  Pallas kernels  233 us (70%)
  blocking collectives  53 us (16%)
  other arithmetic  38.8 us (12%)
  between operations  4.08 us (1%)
    pallas_call x1, Pallas kernels, local_fast(): pl.pallas_call(predict_kernel, out_shape=(jax.ShapeDtypeStruct((2, shot_b...  233 us
    psum x1, blocking collectives, local_fast(): both = lax.psum(both, ('row', 'col'))  53 us
    convert_element_type x1, other arithmetic, local_fast(): out_re = (field[0].astype(jnp.float32) - sub_re).astype(jnp.bfloat16)  12.2 us
    reduce_sum x1, other arithmetic, local_fast(): local_data = jnp.sum(jnp.square(field.astype(jnp.float32)))  8.37 us

profile of v1, /device:TPU:0, one launch (start us, length us, event | category | flops | bytes accessed | tf_op | source)
XLA Modules:
  0.0 330.8 jit_solution(259316781057060438)
XLA Ops:
  0.0 0.0 copy-start
  0.0 0.0 copy-start.1
  0.0 8.4 %multiply_reduce_fusion = f32[]{:T(128)} fusion(bf16[2,1,2048,1024]{3,2,1,0:T(8,128)(2,1)} %param.3), kind=kLoop, calls=%fused_computation | loop fusion | flops 12582911 | bytes 8388612 | tf_op jit(solution)/shard_map/reduce_sum | solution.py:313
  8.4 0.0 copy-done.1
  8.4 0.6 fusion.13
  10.9 0.0 copy-done
  11.0 0.2 fusion.2
  11.2 0.2 fusion.4
  11.4 4.8 %dynamic-slice_select_fusion.2 = (bf16[2,1,512,1024]{3,2,0,1:T(8,128)(2,1)S(1)}, bf16[2,1,512,1024]{3,2,0,1:T(8,128)(2,1)S(1)}, bf16[2,1,512,1024]{3,2,0,1:T(8,128)(2,1)S(1)}) fusion(bf16[2,1,2048,1024]{3,2,0,1:T(8,128)(2,1)} %bitcast.39, s32[]{:T(128)S(6)} %select_n.69, pred[]{:T(512)S(6)} %eq.13, s32[]{:T(128)S(6)} %select_n.81, pred[]{:T(512)S(6)} %eq.15, ...), kind=kLoop, calls=%fused_computation.12 | loop fusion | flops 3145728 | bytes 12582927 | tf_op jit(solution)/shard_map/jit(_where)/select_n | solution.py:287
  16.2 0.2 copy.15
  16.4 0.5 copy_bitcast_fusion
  16.9 5.0 %pad_maximum_fusion.pieces = bf16[24,2,64,1024]{3,2,1,0:T(8,128)(2,1)} fusion(bf16[8,2,64,1024]{3,2,1,0:T(8,128)(2,1)S(1)} %get-tuple-element.19, bf16[8,2,64,1024]{3,2,1,0:T(8,128)(2,1)S(1)} %get-tuple-element.20, bf16[8,2,64,1024]{3,2,1,0:T(8,128)(2,1)S(1)} %bitcast.41), kind=kLoop, calls=%fused_computation.6 | loop fusion | flops 6291456 | bytes 12582912 | tf_op jit(solution)/shard_map/concatenate | solution.py:290
  21.9 232.6 %predict.1 = (f32[2,2048,1024]{2,1,0:T(8,128)}, f32[8,1024]{1,0:T(8,128)}) custom-call(bf16[24,2,64,1024]{3,2,1,0:T(8,128)(2,1)} %pad_maximum_fusion.pieces), custom_call_target="tpu_custom_call" | custom-call | tf_op jit(solution)/shard_map/predict/pallas_call | solution.py:293
  254.5 1.4 reduce_sum.19
  256.6 0.7 pad_maximum_fusion.1
  257.3 53.0 %psum.7 = f32[2]{0:T(128)S(1)} all-reduce(f32[2]{0:T(128)S(1)} %pad_maximum_fusion.1), channel_id=1, replica_groups=mesh['row'=4,'col'=8] {'row','col'}, use_global_device_ids=true, to_apply=%region_2.3 | all-reduce | flops 2 | bytes 16 | tf_op jit(solution)/shard_map/psum | solution.py:315
  310.2 0.6 fusion.12
  312.3 12.2 %fusion.1 = (bf16[1,2048,1024]{2,1,0:T(8,128)(2,1)S(1)}, bf16[1,2048,1024]{2,1,0:T(8,128)(2,1)}) fusion(f32[2,2048,1024]{2,1,0:T(8,128)} %get-tuple-element.8, f32[1024]{0:T(1024)S(1)} %get-tuple-element.21, f32[1024]{0:T(1024)S(1)} %get-tuple-element.22, f32[]{:T(128)} %bitcast.15, bf16[2,1,2048,1024]{3,2,1,0:T(8,128)(2,1)} %param.3), kind=kLoop, calls=%fused_computation.5 | loop fusion | flops 29360128 | bytes 33562628 | tf_op jit(solution)/shard_map/convert_element_type | solution.py:322
  324.4 6.3 %maximum_bitcast_fusion = bf16[2,1,2048,1024]{3,2,1,0:T(8,128)(2,1)} fusion(bf16[1,2048,1024]{2,1,0:T(8,128)(2,1)} %get-tuple-element.10, bf16[1,2048,1024]{2,1,0:T(8,128)(2,1)S(1)} %get-tuple-element.9), kind=kLoop, calls=%fused_computation.1 | loop fusion | flops 4194304 | bytes 16777216 | tf_op jit(solution)/shard_map/broadcast_in_dim | solution.py:324
  (1 shorter events, 0.0 us)
Async XLA Ops:
  0.0 10.9 %copy-start = (f32[11,1024]{1,0:T(8,128)S(1)}, f32[11,1024]{1,0:T(8,128)}, u32[]{:S(2)}) copy-start(f32[11,1024]{1,0:T(8,128)} %param.5) | copy-start | bytes 135172
  0.0 8.4 %copy-start.1 = (s32[16]{0:T(128)S(1)}, s32[16]{0:T(128)}, u32[]{:S(2)}) copy-start(s32[16]{0:T(128)} %param.4) | copy-start | bytes 196

commit v2 on v1

--- a/solution.py
+++ b/solution.py
@@ -17,10 +17,13 @@
 
 CHUNK = 64
 NCHUNK = STEPS * PANEL // CHUNK
-GROUP = 4
+GROUP = 256 // CHUNK
 NGROUP = NCHUNK // GROUP
 TILE = 256
-LAG = 5
+HOP = 1
+LAG = 5 * HOP
+AHEAD = 2
+STRIP = 64
 
 
 def spread(block, axis, holder):
@@ -91,8 +94,14 @@
     return result.astype(jnp.bfloat16)
 
 
-def predict_kernel(pieces, mult, energy, own, first, second, left, acc, right,
-                   xs, xr, ys, yr, us, ds, zr, ps, pr, own_sem, out_sem):
+def predict_kernel(piece0, piece1, piece2, field, mult, gain,
+                   own, first, second, left, acc, right, energy, strip, part_sums, row_sums, col_sums,
+                   xs, xr, ys, yr, us, ds, zr, ps, pr, own_sem, out_sem, strip_sem,
+                   rs, rr, cs, cr):
+    panels = (piece0, piece1, piece2)
+    per_panel = PANEL // CHUNK
+    count = 2.0 * SIDE * SIDE
+    factor = 1.0 / math.sqrt(STEPS * PANEL)
     row = lax.axis_index("row")
     col = lax.axis_index("col")
     z = col // 2
@@ -104,28 +113,39 @@
     above = z - row
     far = jnp.abs(above)
 
-    load = pltpu.make_async_copy(pieces, own, own_sem)
-    load.start()
+    loads = [
+        pltpu.make_async_copy(panels[t], own.at[pl.ds(t * per_panel, per_panel)], own_sem.at[t])
+        for t in range(STEPS)
+    ]
+    for load in loads:
+        load.start()
+
+    def strip_copy(s):
+        return pltpu.make_async_copy(
+            field.at[:, pl.ds(pl.multiple_of(s * STRIP, STRIP), STRIP), :],
+            strip.at[s % 2], strip_sem.at[s % 2])
+
+    nstrip = field.shape[1] // STRIP
+    strip_copy(0).start()
+    energy[...] = jnp.zeros_like(energy)
     barrier = pltpu.get_barrier_semaphore()
-    pl.semaphore_signal(barrier, inc=1, device_id=(along_x, col), device_id_type=MESH)
-    pl.semaphore_signal(barrier, inc=1, device_id=(along_y, col), device_id_type=MESH)
-    pl.semaphore_signal(barrier, inc=1, device_id=(row, partner), device_id_type=MESH)
-
-    @pl.when(z > 0)
-    def _():
-        pl.semaphore_signal(barrier, inc=1, device_id=(row, col - 2), device_id_type=MESH)
-
-    @pl.when(z < 3)
-    def _():
-        pl.semaphore_signal(barrier, inc=1, device_id=(row, col + 2), device_id_type=MESH)
-
-    pl.semaphore_wait(barrier, 3 + jnp.minimum(z, 1) + jnp.minimum(3 - z, 1))
-
-    def x_copy(k):
+    for j in range(1, 4):
+        pl.semaphore_signal(barrier, inc=1, device_id=((row + j) % 4, col), device_id_type=MESH)
+    for j in range(1, 8):
+        pl.semaphore_signal(barrier, inc=1, device_id=(row, (col + j) % 8), device_id_type=MESH)
+    pl.semaphore_wait(barrier, 10)
+
+    def x_copy(t, k):
         to = along_x + (k % 2) * (along_y - along_x)
         return pltpu.make_async_remote_copy(
-            src_ref=pieces.at[k], dst_ref=first.at[k], send_sem=xs.at[k], recv_sem=xr.at[k],
-            device_id=(to, col), device_id_type=MESH)
+            src_ref=panels[t].at[k - t * per_panel], dst_ref=first.at[k], send_sem=xs.at[k],
+            recv_sem=xr.at[k], device_id=(to, col), device_id_type=MESH)
+
+    def x_start(k):
+        for t in range(STEPS):
+            @pl.when(jnp.logical_and(k >= t * per_panel, k < (t + 1) * per_panel))
+            def _():
+                x_copy(t, k).start()
 
     def y_copy(k):
         to = along_y + (k % 2) * (along_x - along_y)
@@ -157,11 +177,12 @@
 
         p_copy(src, k).start()
 
-    @pl.loop(0, NCHUNK)
+    @pl.loop(0, AHEAD)
     def _(k):
-        x_copy(k).start()
-
-    load.wait()
+        x_start(k)
+
+    for load in loads:
+        load.wait()
 
     def out_copy(part, at):
         return pltpu.make_async_copy(
@@ -171,11 +192,15 @@
     def _(s):
         @pl.when(s < NCHUNK)
         def _():
-            x_copy(s).wait_recv()
+            x_start(s + AHEAD)
+            arrival = pltpu.make_async_remote_copy(
+                src_ref=second.at[s], dst_ref=first.at[s], send_sem=xs.at[s], recv_sem=xr.at[s],
+                device_id=(along_x, col), device_id_type=MESH)
+            arrival.wait_recv()
             first[s] = first[s] + own[s]
             y_copy(s).start()
 
-        k1 = s - 1
+        k1 = s - HOP
 
         @pl.when(jnp.logical_and(k1 >= 0, k1 < NCHUNK))
         def _():
@@ -187,7 +212,7 @@
                 pass_on(second.at[k1], k1)
                 left[core, k1] = second[k1]
 
-        k2 = s - 1 - far
+        k2 = s - HOP * (1 + far)
 
         @pl.when(jnp.logical_and(far > 0, jnp.logical_and(k2 >= 0, k2 < NCHUNK)))
         def _():
@@ -201,6 +226,17 @@
             pltpu.make_async_remote_copy(
                 src_ref=second.at[k3], dst_ref=left.at[1 - core, k3], send_sem=ps.at[k3],
                 recv_sem=pr.at[k3], device_id=(row, partner), device_id_type=MESH).wait_recv()
+
+        @pl.when(s < nstrip)
+        def _():
+            strip_copy(s).wait()
+
+            @pl.when(s + 1 < nstrip)
+            def _():
+                strip_copy(s + 1).start()
+
+            value = strip[s % 2].astype(jnp.float32)
+            energy[0] = energy[0] + jnp.sum((value * value).reshape(2 * STRIP // 8, 8, width), axis=0)
 
         step = s - (LAG + GROUP - 1)
 
@@ -238,29 +274,32 @@
                     def _():
                         acc[c, pl.ds(at, TILE), :] = got
 
-                    @pl.when(group > 0)
+                    @pl.when(jnp.logical_and(group > 0, group < NGROUP - 1))
                     def _():
                         acc[c, pl.ds(at, TILE), :] = acc[c, pl.ds(at, TILE), :] + got
+
+                    @pl.when(group == NGROUP - 1)
+                    def _():
+                        value = (acc[c, pl.ds(at, TILE), :] + got) * factor
+                        acc[c, pl.ds(at, TILE), :] = value
+                        energy[1] = energy[1] + jnp.sum(
+                            (value * value).reshape(TILE // 8, 8, width), axis=0)
 
                 @pl.when(group == NGROUP - 1)
                 def _():
                     for c in range(2):
                         out_copy(c, at).start()
 
-    energy[...] = jnp.zeros_like(energy)
-
-    @pl.loop(0, acc.shape[1] // 8)
-    def _(i):
-        at = pl.multiple_of(i * 8, 8)
-        re = acc[0, pl.ds(at, 8), :]
-        im = acc[1, pl.ds(at, 8), :]
-        energy[...] = energy[...] + (re * re + im * im)
-
-    pltpu.make_async_copy(acc, mult, out_sem.at[0]).wait()
+    sums = energy[:, :, :128]
+    for j in range(1, width // 128):
+        sums = sums + energy[:, :, j * 128:(j + 1) * 128]
+    part_sums[0] = sums
 
     @pl.loop(0, NCHUNK)
     def _(k):
-        x_copy(k).wait_send()
+        pltpu.make_async_remote_copy(
+            src_ref=own.at[k], dst_ref=first.at[k], send_sem=xs.at[k], recv_sem=xr.at[k],
+            device_id=(along_x, col), device_id_type=MESH).wait_send()
         y_copy(k).wait_send()
         p_copy(second.at[k], k).wait_send()
 
@@ -271,13 +310,41 @@
         @pl.when(go_down)
         def _():
             z_copy(second.at[k], k, col - 2, ds).wait_send()
+
+    row_copies = [
+        pltpu.make_async_remote_copy(
+            src_ref=part_sums.at[0], dst_ref=row_sums.at[j - 1], send_sem=rs.at[j - 1],
+            recv_sem=rr.at[j - 1], device_id=((row + j) % 4, col), device_id_type=MESH)
+        for j in range(1, 4)
+    ]
+    for copy in row_copies:
+        copy.start()
+    for j in range(3):
+        row_copies[j].wait_recv()
+        sums = sums + row_sums[j]
+    part_sums[1] = sums
+    col_copies = [
+        pltpu.make_async_remote_copy(
+            src_ref=part_sums.at[1], dst_ref=col_sums.at[j - 1], send_sem=cs.at[j - 1],
+            recv_sem=cr.at[j - 1], device_id=(row, (col + j) % 8), device_id_type=MESH)
+        for j in range(1, 8)
+    ]
+    pltpu.make_async_copy(acc, mult, out_sem.at[0]).wait()
+    for copy in col_copies:
+        copy.start()
+    for j in range(7):
+        col_copies[j].wait_recv()
+        sums = sums + col_sums[j]
+    data = jnp.full((8, 128), jnp.sum(sums[0]), jnp.float32)
+    predicted = jnp.full((8, 128), jnp.sum(sums[1]), jnp.float32)
+    gain[...] = jnp.sqrt((data / count + 1e-05) / (predicted / count + 1e-05))
+    for copy in row_copies + col_copies:
+        copy.wait_send()
 
 
 def local_fast(wavefield, panel_order, filter_taps):
     shot_block = wavefield.shape[2]
     recv_block = wavefield.shape[3]
-    factor = 1.0 / math.sqrt(STEPS * PANEL)
-    count = 2.0 * SIDE * SIDE
     field = wavefield[:, 0]
     me = lax.axis_index("row")
     parts = []
@@ -287,16 +354,15 @@
         piece = jnp.where(me == start // shot_block, piece, jnp.zeros_like(piece))
         piece = piece.reshape(2, PANEL // CHUNK, CHUNK, recv_block)
         parts.append(jnp.swapaxes(piece, 0, 1))
-    pieces = jnp.concatenate(parts, axis=0)
     block = (NCHUNK, 2, CHUNK, recv_block)
     dma = pltpu.SemaphoreType.DMA
-    mult, energy = pl.pallas_call(
+    mult, gain = pl.pallas_call(
         predict_kernel,
         out_shape=(
             jax.ShapeDtypeStruct((2, shot_block, recv_block), jnp.float32),
-            jax.ShapeDtypeStruct((8, recv_block), jnp.float32),
+            jax.ShapeDtypeStruct((8, 128), jnp.float32),
         ),
-        in_specs=[pl.BlockSpec(memory_space=pl.ANY)],
+        in_specs=[pl.BlockSpec(memory_space=pl.ANY)] * 4,
         out_specs=(pl.BlockSpec(memory_space=pl.ANY), pl.BlockSpec(memory_space=pltpu.VMEM)),
         scratch_shapes=[
             pltpu.VMEM(block, jnp.bfloat16),
@@ -305,23 +371,23 @@
             pltpu.VMEM((2,) + block, jnp.bfloat16),
             pltpu.VMEM((2, shot_block, recv_block), jnp.float32),
             pltpu.VMEM((2, GROUP, 2, CHUNK, recv_block), jnp.bfloat16),
-        ] + [dma((NCHUNK,))] * 9 + [dma, dma((1,))],
+            pltpu.VMEM((2, 8, recv_block), jnp.float32),
+            pltpu.VMEM((2, 2, STRIP, recv_block), jnp.bfloat16),
+            pltpu.VMEM((2, 2, 8, 128), jnp.float32),
+            pltpu.VMEM((3, 2, 8, 128), jnp.float32),
+            pltpu.VMEM((7, 2, 8, 128), jnp.float32),
+        ] + [dma((NCHUNK,))] * 9 + [
+            dma((STEPS,)), dma((1,)), dma((2,)), dma((3,)), dma((3,)), dma((7,)), dma((7,))],
         compiler_params=pltpu.CompilerParams(
             collective_id=0, has_side_effects=True, vmem_limit_bytes=60 << 20),
         name="predict",
-    )(pieces)
-    local_data = jnp.sum(jnp.square(field.astype(jnp.float32)))
-    both = jnp.stack([local_data, jnp.sum(energy) * (factor * factor)])
-    both = lax.psum(both, ("row", "col"))
-    gain = jnp.sqrt((both[0] / count + 1e-05) / (both[1] / count + 1e-05))
+    )(*parts, field)
+    scale = gain[0, 0]
     spec_re, spec_im = frequency_spectrum(filter_taps, 1)
-    mult_re = mult[0] * factor
-    mult_im = mult[1] * factor
-    sub_re = gain * (spec_re * mult_re - spec_im * mult_im)
-    sub_im = gain * (spec_re * mult_im + spec_im * mult_re)
-    out_re = (field[0].astype(jnp.float32) - sub_re).astype(jnp.bfloat16)
-    out_im = (field[1].astype(jnp.float32) - sub_im).astype(jnp.bfloat16)
-    return jnp.stack([out_re, out_im])[:, None]
+    same = jnp.stack([spec_re, spec_re])
+    cross = jnp.stack([-spec_im, spec_im])
+    moved = scale * (same * mult + cross * mult[::-1])
+    return (field.astype(jnp.float32) - moved).astype(jnp.bfloat16)[:, None]
 
 
 def solution(mesh):

time: 332 us -> 228 us (0.69)
  blocking collectives: 53 us -> 0 us
  Pallas kernels: 233 us -> 195 us
  other arithmetic: 38.8 us -> 23.3 us
  local copies, waits for them, and re-layouts: 1.91 us -> 6.9 us
    psum x1 -> x0, blocking collectives: 53 us -> none  [local_fast(): both = lax.psum(both, ('row', 'col'))]
    pallas_call x1, Pallas kernels: 233 us -> 195 us  [local_fast(): pl.pallas_call(predict_kernel, out_shape=(jax.ShapeDtypeStruct((2, shot_b...]
    convert_element_type x1 -> x0, other arithmetic: 12.2 us -> none  [local_fast(): out_re = (field[0].astype(jnp.float32) - sub_re).astype(jnp.bfloat16)]
    broadcast_in_dim x1, other arithmetic: 6.35 us -> 18.5 us  [local_fast(): return (field.astype(jnp.float32) - moved).astype(jnp.bfloat16)[:, None]]
    reduce_sum x2 -> x0, other arithmetic: 9.74 us -> none  [the longest x1 8.37 us: local_fast(): local_data = jnp.sum(jnp.square(field.astype(jnp.float32)))]
    concatenate x1 -> x0, other arithmetic: 4.98 us -> none  [local_fast(): pieces = jnp.concatenate(parts, axis=0)]
where the time goes in v2:
time: 228 us
  Pallas kernels  195 us (86%)
  other arithmetic  23.3 us (10%)
  local copies, waits for them, and re-layouts  6.9 us (3%)
    pallas_call x1, Pallas kernels, local_fast(): pl.pallas_call(predict_kernel, out_shape=(jax.ShapeDtypeStruct((2, shot_b...  195 us
    broadcast_in_dim x1, other arithmetic, local_fast(): return (field.astype(jnp.float32) - moved).astype(jnp.bfloat16)[:, None]  18.5 us
    select_n x1, other arithmetic, local_fast(): piece = jnp.where(me == start // shot_block, piece, jnp.zeros_like(piece))  4.81 us

profile of v2, /device:TPU:0, one launch (start us, length us, event | category | flops | bytes accessed | tf_op | source)
XLA Modules:
  0.0 228.0 jit_solution(2441488913553779644)
XLA Ops:
  0.0 0.0 copy-start
  0.0 1.4 fusion.10
  3.4 0.0 copy-done
  3.5 0.2 fusion.1
  3.7 0.2 convolution_bitcast_fusion
  3.9 4.8 %dynamic-slice_select_fusion = (bf16[2,1,512,1024]{3,2,0,1:T(8,128)(2,1)S(1)}, bf16[2,1,512,1024]{3,2,0,1:T(8,128)(2,1)S(1)}, bf16[2,1,512,1024]{3,2,0,1:T(8,128)(2,1)S(1)}) fusion(bf16[2,1,2048,1024]{3,2,0,1:T(8,128)(2,1)} %bitcast.43, s32[]{:T(128)S(6)} %select_n.81, pred[]{:T(512)S(6)} %eq.15, s32[]{:T(128)S(6)} %select_n.75, pred[]{:T(512)S(6)} %eq.14, ...), kind=kLoop, calls=%fused_computation.5 | loop fusion | flops 3145728 | bytes 12582927 | tf_op jit(solution)/shard_map/jit(_where)/select_n | solution.py:354
  8.7 2.6 %copy_bitcast_fusion = (bf16[8,2,64,1024]{3,2,1,0:T(8,128)(2,1)}, bf16[8,2,64,1024]{3,2,1,0:T(8,128)(2,1)}) fusion(bf16[2,8,64,1024]{3,2,1,0:T(8,128)(2,1)S(1)} %bitcast.47, bf16[2,8,64,1024]{3,2,1,0:T(8,128)(2,1)S(1)} %bitcast.48), kind=kLoop, calls=%fused_computation.2 | loop fusion | bytes 8388608 | tf_op jit(solution)/shard_map/transpose | solution.py:356
  11.4 1.6 copy.15
  12.9 195.3 %predict.1 = (f32[2,2048,1024]{2,1,0:T(8,128)}, f32[8,128]{1,0:T(8,128)}) custom-call(bf16[8,2,64,1024]{3,2,1,0:T(8,128)(2,1)} %bitcast.45, bf16[8,2,64,1024]{3,2,1,0:T(8,128)(2,1)} %get-tuple-element.16.piece1, bf16[8,2,64,1024]{3,2,1,0:T(8,128)(2,1)} %get-tuple-element.15.piece2, bf16[2,2048,1024]{2,1,0:T(8,128)(2,1)} %bitcast.44), custom_call_target="tpu_custom_call" | custom-call | tf_op jit(solution)/shard_map/predict/pallas_call | solution.py:359
  208.3 1.3 slice.15
  209.5 18.5 %fusion = bf16[2,1,2048,1024]{3,2,1,0:T(8,128)(2,1)} fusion(f32[2,2048,1024]{2,1,0:T(8,128)} %get-tuple-element.8, f32[2,1024]{1,0:T(2,128)S(1)} %get-tuple-element.18, f32[2,1024]{1,0:T(2,128)S(1)} %get-tuple-element.17, f32[]{:T(128)} %bitcast.13, bf16[2,1,2048,1024]{3,2,1,0:T(8,128)(2,1)} %param.3), kind=kLoop, calls=%fused_computation.1 | loop fusion | flops 29360128 | bytes 33570820 | tf_op jit(solution)/shard_map/broadcast_in_dim | solution.py:390
  (2 shorter events, 0.0 us)
Async XLA Ops:
  0.0 3.4 %copy-start = (f32[11,1024]{1,0:T(8,128)S(1)}, f32[11,1024]{1,0:T(8,128)}, u32[]{:S(2)}) copy-start(f32[11,1024]{1,0:T(8,128)} %param.5) | copy-start | bytes 135172
